TPU v7x, 512 devices: a whole 4x4x16 slice. The times are simulated.
512 devices in a mesh: prow: 32 (over y, x, core), pcol: 16 (over z).
Axes of the slice: x: 4, y: 4, z: 16, core: 2. Of those that a mesh axis runs over, the one named last changes fastest.
Arguments:
- inverse_blocks: bfloat16 [128, 128, 128, 128], P('pcol', 'prow'), may hold values from -6 to 6
- lower_blocks: bfloat16 [128, 4, 128, 128], P('prow', None, 'pcol'), may hold values from -0.625 to 0.625
- pattern: int32 [4, 64], replicated, may hold values from 0 to 127, as said below
- diag_inverse: float32 [4, 16384], P(None, ('prow', 'pcol')), may hold values from -6 to 6
Outputs:
- inverse_column: float32 [128, 4, 128, 128], P('pcol', None, 'prow')
- inverse_diag: float32 [4, 16384], P(None, ('prow', 'pcol'))
Inputs may be any that keep to these rules, and one draw needn't show every extreme that they name: `pattern`: each row names 64 different ancestor blocks.
All inputs are finite; a program needn't handle non-finite values.
Results may differ from a plain program's by a relative error of at most 0.0003.
Values may be sent and summed in bfloat16 or wider, within the bound.
A program may use at most 64 MiB of HBM per device.

v0:
```python
import jax
import jax.numpy as jnp
from jax import lax
from jax.sharding import PartitionSpec as P


def broadcast(x, axis, root):
    mine = lax.axis_index(axis) == root
    return lax.psum(jnp.where(mine, x, jnp.zeros_like(x)), axis)


def per_device(inverse_blocks, lower_blocks, pattern, diag_inverse):
    blocks_i = inverse_blocks.shape[0]
    blocks_j = inverse_blocks.shape[1]
    block_width = inverse_blocks.shape[3]
    node_count = lower_blocks.shape[1]
    row_groups = lax.axis_size("prow")
    col_groups = lax.axis_size("pcol")
    block_count = blocks_j * row_groups
    ratio = row_groups // col_groups
    row_share = block_width // row_groups
    matches = pattern[None, :, :] == jnp.arange(block_count, dtype=jnp.int32)[:, None, None]
    present = jnp.sum(matches.astype(jnp.float32), axis=2)
    start_j = lax.axis_index("prow") * blocks_j
    start_i = lax.axis_index("pcol") * blocks_i
    keep_j = lax.dynamic_slice_in_dim(present, start_j, blocks_j, 0)
    keep_i = lax.dynamic_slice_in_dim(present, start_i, blocks_i, 0)
    whole = lax.all_gather(lower_blocks, "pcol", axis=2, tiled=True)
    masked = whole * keep_j.astype(jnp.bfloat16)[:, :, None, None]
    summed = lax.psum_scatter(
        jnp.einsum("ijrb,jkbe->rike", inverse_blocks, masked, preferred_element_type=jnp.float32),
        "prow",
        scatter_dimension=0,
        tiled=True,
    )
    column = summed * (-keep_i)[None, :, :, None]
    row_begin = lax.axis_index("prow") * row_share
    pieces = []
    for offset in range(ratio):
        received = broadcast(masked, "prow", lax.axis_index("pcol") * ratio + offset)
        pieces.append(lax.dynamic_slice_in_dim(received, row_begin, row_share, 2))
    own_lower = jnp.concatenate(pieces, axis=0)
    partial_value = jnp.einsum(
        "ikra,rikb->kab", own_lower.astype(jnp.float32), column, precision=lax.Precision.HIGHEST
    )
    partial_value = partial_value.reshape(node_count, block_width * block_width)
    totals = lax.psum(partial_value, ("prow", "pcol"))
    piece_len = block_width * block_width // (row_groups * col_groups)
    flat_index = lax.axis_index("prow") * col_groups + lax.axis_index("pcol")
    diag_piece = lax.dynamic_slice_in_dim(totals, flat_index * piece_len, piece_len, 1)
    return (jnp.transpose(column, (1, 2, 0, 3)), diag_inverse - diag_piece)


def solution(mesh):
    placed = (
        P("pcol", "prow", None, None),
        P("prow", None, "pcol", None),
        P(),
        P(None, ("prow", "pcol")),
    )
    return jax.shard_map(
        per_device,
        mesh=mesh,
        in_specs=placed,
        out_specs=(P("pcol", None, "prow", None), P(None, ("prow", "pcol"))),
        check_vma=False,
    )
```

profile of v0, /device:TPU:1, one launch (start us, length us, event | category | flops | bytes accessed | tf_op | source)
XLA Modules:
  0.0 765.5 jit_solution(11507525416745244874)
XLA Ops:
  7.2 0.0 copy-start
  7.2 0.0 all-reduce.6.cloned.1.call-start
  7.2 0.9 convert_reduce_fusion
  8.1 0.8 copy.15
  8.9 31.8 %all_gather.3 = bf16[4,4,128,128]{3,0,2,1:T(4,128)(2,1)S(1)} all-gather(bf16[4,4,8,128]{3,0,2,1:T(4,128)(2,1)S(1)} %copy.15), channel_id=1, replica_groups=mesh['prow'=32,'pcol'=16] {'pcol'}, dimensions={2}, use_global_device_ids=true | all-gather | bytes 557056 | tf_op jit(solution)/shard_map/all_gather | solution.py:28
  40.7 0.1 dynamic-slice_convert_fusion
  40.8 1.6 broadcast_select_fusion.1
  42.4 0.0 all-reduce.6.cloned.1.call-update
  42.4 0.0 reduce-scatter.2.cloned.1.call-start
  42.5 0.0 copy-done
  42.5 1.8 convolution_bitcast_fusion
  44.3 2.0 copy.17
  46.3 0.0 copy-start.1
  46.3 0.0 reduce-scatter.2.cloned.1.call-update
  46.4 0.0 all-reduce.4.cloned.1.call-start
  46.4 0.1 dynamic-slice_negate_fusion
  46.5 135.4 %all-reduce.6.cloned.1.call-done = (bf16[4,4,128,128]{3,0,2,1:T(4,128)(2,1)}, bf16[4,4,128,128]{3,0,2,1:T(4,128)(2,1)}) async-done(((bf16[4,4,128,128]{3,0,2,1:T(4,128)(2,1)}, bf16[4,4,128,128]{3,0,2,1:T(4,128)(2,1)}), (bf16[4,4,128,128]{3,0,2,1:T(4,128)(2,1)}, bf16[4,4,128,128]{3,0,2,1:T(4,128)(2,1)})) %all-reduce.6.cloned.1.call-update) | async-done | bytes 1048592 | tf_op jit(solution)/shard_map/psum | solution.py:9
  181.9 0.7 constant_dynamic-slice_fusion
  182.6 103.9 %reduce-scatter.2.cloned.1.call-done = f32[4,8,4,128]{3,1,2,0:T(8,128)} async-done(((f32[128,8,4,128]{3,1,2,0:T(8,128)}), f32[4,8,4,128]{3,1,2,0:T(8,128)}) %reduce-scatter.2.cloned.1.call-update) | async-done | bytes 65552 | tf_op jit(solution)/shard_map/reduce_scatter | solution.py:30
  286.5 1.2 convolution_bitcast_fusion.1
  287.7 0.9 copy.31
  288.6 0.0 all-reduce.4.cloned.1.call-update
  288.6 0.9 fusion.7
  289.5 0.7 copy.19
  290.2 467.5 %all-reduce.4.cloned.1.call-done = f32[4,16384]{1,0:T(4,128)} async-done(((f32[4,16384]{1,0:T(4,128)}), f32[4,16384]{1,0:T(4,128)}) %all-reduce.4.cloned.1.call-update) | async-done | bytes 262160 | tf_op jit(solution)/shard_map/psum | solution.py:47
  757.7 0.0 copy-done.1
  757.7 1.3 dynamic-slice_subtract_fusion
Async XLA Ops:
  7.2 35.3 %copy-start = (bf16[8,4,128,128]{3,2,1,0:T(8,128)(2,1)S(1)}, bf16[8,4,128,128]{3,2,1,0:T(8,128)(2,1)}, u32[]{:S(2)}) copy-start(bf16[8,4,128,128]{3,2,1,0:T(8,128)(2,1)} %param.4) | copy-start | bytes 3145732
  7.2 174.7 %all-reduce.6.cloned.1.call-start = ((), (), s32[]{:S(2)}) async-start(), calls=%async_computation.3 | async-start | bytes 2097152 | tf_op jit(solution)/shard_map/psum | solution.py:9
  42.4 244.1 %reduce-scatter.2.cloned.1.call-start = ((), (), s32[]{:S(2)}) async-start(), calls=%async_computation.1 | async-start | bytes 2162688 | tf_op jit(solution)/shard_map/reduce_scatter | solution.py:30
  46.3 711.3 %copy-start.1 = (f32[4,32]{1,0:T(4,128)S(1)}, f32[4,32]{1,0:T(4,128)}, u32[]{:S(2)}) copy-start(f32[4,32]{1,0:T(4,128)} %param.7) | copy-start | bytes 1540
  46.4 711.3 %all-reduce.4.cloned.1.call-start = ((), (), s32[]{:S(2)}) async-start(), calls=%async_computation.2 | async-start | bytes 524288 | tf_op jit(solution)/shard_map/psum | solution.py:47
Sparse Core Ops, SparseCore 0:
  42.5 139.2 all-reduce.5
  186.3 100.2 reduce-scatter.1
  292.0 465.6 all-reduce.3
where the time goes:
time: 767 us; the launch traced here: 766 us
  waiting for transfers between devices  707 us (92%)
  blocking collectives  31.8 us (4%)
  between operations  13.8 us (2%)
    psum x1, waiting for transfers between devices, per_device(): totals = lax.psum(partial_value, ('prow', 'pcol'))  467 us
    psum x1, waiting for transfers between devices, broadcast(): return lax.psum(jnp.where(mine, x, jnp.zeros_like(x)), axis)  135 us
    reduce_scatter x1, waiting for transfers between devices, per_device(): lax.psum_scatter(jnp.einsum('ijrb,jkbe->rike', inverse_blocks, masked, pr...  104 us
    all_gather x1, blocking collectives, per_device(): whole = lax.all_gather(lower_blocks, 'pcol', axis=2, tiled=True)  31.8 us
  transfers between devices with their start and end apart: 3, of which 3 were waited for; matrix products, arithmetic and copies ran while one was open for 1% of the time, Pallas kernels for 0%

commit v1 on v0

v1 whole, which is shorter than its diff:
```python
import jax
import jax.numpy as jnp
from jax import lax
from jax.sharding import PartitionSpec as P


def per_device(inverse_blocks, lower_blocks, pattern, diag_inverse):
    blocks_i = inverse_blocks.shape[0]
    blocks_j = inverse_blocks.shape[1]
    block_width = inverse_blocks.shape[3]
    node_count = lower_blocks.shape[1]
    row_groups = lax.axis_size("prow")
    col_groups = lax.axis_size("pcol")
    block_count = blocks_j * row_groups
    ratio = row_groups // col_groups
    row_share = block_width // row_groups
    p = lax.axis_index("prow")
    c = lax.axis_index("pcol")
    matches = pattern[None, :, :] == jnp.arange(block_count, dtype=jnp.int32)[:, None, None]
    present = jnp.sum(matches.astype(jnp.float32), axis=2)
    keep_j = lax.dynamic_slice_in_dim(present, p * blocks_j, blocks_j, 0)
    keep_i = lax.dynamic_slice_in_dim(present, c * blocks_i, blocks_i, 0)
    shard = lower_blocks * keep_j.astype(jnp.bfloat16)[:, :, None, None]
    pieces = []
    for flip in range(ratio):
        moves = [
            ((ratio * q + k) * col_groups + z, (ratio * z + (k ^ flip)) * col_groups + q)
            for q in range(col_groups)
            for k in range(ratio)
            for z in range(col_groups)
        ]
        start = ((p % ratio) ^ flip) * row_share
        piece = lax.dynamic_slice_in_dim(shard, start, row_share, 2)
        pieces.append(lax.ppermute(piece, ("prow", "pcol"), moves))
    whole = lax.all_gather(lower_blocks, "pcol", axis=2, tiled=True)
    masked = whole * keep_j.astype(jnp.bfloat16)[:, :, None, None]
    summed = lax.psum_scatter(
        jnp.einsum("ijrb,jkbe->rike", inverse_blocks, masked, preferred_element_type=jnp.float32),
        "prow",
        scatter_dimension=0,
        tiled=True,
    )
    column = summed * (-keep_i)[None, :, :, None]
    first = (p % ratio) == 0
    own_lower = jnp.concatenate(
        [jnp.where(first, pieces[0], pieces[1]), jnp.where(first, pieces[1], pieces[0])], axis=0
    )
    partial_value = jnp.einsum(
        "ikra,rikb->kab", own_lower.astype(jnp.float32), column, precision=lax.Precision.HIGHEST
    )
    partial_value = partial_value.reshape(node_count, block_width * block_width)
    diag_piece = lax.psum_scatter(partial_value, ("prow", "pcol"), scatter_dimension=1, tiled=True)
    return (jnp.transpose(column, (1, 2, 0, 3)), diag_inverse - diag_piece)


def solution(mesh):
    placed = (
        P("pcol", "prow", None, None),
        P("prow", None, "pcol", None),
        P(),
        P(None, ("prow", "pcol")),
    )
    return jax.shard_map(
        per_device,
        mesh=mesh,
        in_specs=placed,
        out_specs=(P("pcol", None, "prow", None), P(None, ("prow", "pcol"))),
        check_vma=False,
    )
```

time: 767 us -> 2730 us (3.56)
  waiting for transfers between devices: 707 us -> 2630 us
    unnamed x3, waiting for transfers between devices: 0.05 us -> 2540 us
    psum x2 -> x0, waiting for transfers between devices: 603 us -> none  [the longest x1 467 us: per_device(): totals = lax.psum(partial_value, ('prow', 'pcol'))]
  transfers between devices with their start and end apart: 3 -> 4, of which waited for: 3 -> 3; matrix products, arithmetic and copies ran while one was open for 1% -> 0% of each run, Pallas kernels for 0% -> 0%
where the time goes in v1:
time: 2730 us; the launch traced here: 2700 us
  waiting for transfers between devices  2630 us (96%)
  blocking collectives  32 us (1%)
    unnamed x3, waiting for transfers between devices  2540 us
    reduce_scatter x1, waiting for transfers between devices, per_device(): lax.psum_scatter(jnp.einsum('ijrb,jkbe->rike', inverse_blocks, masked, pr...  91.3 us
  transfers between devices with their start and end apart: 4, of which 3 were waited for; matrix products, arithmetic and copies ran while one was open for 0% of the time, Pallas kernels for 0%

profile of v1, /device:TPU:1, one launch (start us, length us, event | category | flops | bytes accessed | tf_op | source)
XLA Modules:
  0.0 2701.8 jit_solution(13334473209895072539)
XLA Ops:
  7.2 0.0 copy-start
  7.2 0.0 reduce-scatter.5.cloned.1.call-start
  7.2 0.9 convert_reduce_fusion
  8.1 0.1 dynamic-slice_convert_fusion
  8.2 0.1 copy.17
  8.3 32.0 %all_gather.3 = bf16[4,4,128,128]{3,2,1,0:T(8,128)(2,1)S(1)} all-gather(bf16[4,4,8,128]{3,2,1,0:T(8,128)(2,1)} %param.5), channel_id=1, replica_groups=mesh['prow'=32,'pcol'=16] {'pcol'}, dimensions={2}, use_global_device_ids=true | all-gather | bytes 557056 | tf_op jit(solution)/shard_map/all_gather | solution.py:35
  40.3 0.0 copy-done
  40.3 1.0 convolution_bitcast_fusion
  41.4 2.1 copy.19
  43.4 0.0 copy-start.1
  43.4 0.0 reduce-scatter.5.cloned.1.call-update
  43.5 0.0 reduce-scatter.7.cloned.1.call-start
  43.5 0.7 copy-done.1
  44.2 0.1 copy_multiply_fusion
  44.3 0.7 collective-permute-start
  45.0 10.2 collective-permute-start.1
  55.2 0.1 dynamic-slice_negate_fusion
  55.2 0.0 collective-permute-done
  55.2 0.7 collective-permute-done.1
  56.0 91.3 %reduce-scatter.5.cloned.1.call-done = f32[4,8,4,128]{3,1,2,0:T(8,128)} async-done(((f32[128,8,4,128]{3,1,2,0:T(8,128)}), f32[4,8,4,128]{3,1,2,0:T(8,128)}) %reduce-scatter.5.cloned.1.call-update) | async-done | bytes 65552 | tf_op jit(solution)/shard_map/reduce_scatter | solution.py:37
  147.3 1.2 convolution_bitcast_fusion.1
  148.5 4.7 copy.30
  153.1 0.0 copy-start.2
  153.1 0.0 copy-start.3
  153.1 0.0 reduce-scatter.7.cloned.1.call-update
  153.1 0.8 copy-done.2
  154.0 0.1 fusion.7
  154.0 0.7 copy.22
  154.7 2538.9 %reduce-scatter.7.cloned.1.call-done = f32[32,4]{1,0:T(8,128)} async-done(((f32[16384,4]{1,0:T(8,128)}), f32[32,4]{1,0:T(8,128)}) %reduce-scatter.7.cloned.1.call-update) | async-done | bytes 528
  2693.6 0.8 copy.29
  2694.4 0.0 copy-done.3
  2694.4 0.6 sub.3
  (2 shorter events, 0.0 us)
Async XLA Ops:
  7.2 33.2 %copy-start = (bf16[8,4,128,128]{3,2,1,0:T(8,128)(2,1)S(1)}, bf16[8,4,128,128]{3,2,1,0:T(8,128)(2,1)}, u32[]{:S(2)}) copy-start(bf16[8,4,128,128]{3,2,1,0:T(8,128)(2,1)} %param.4) | copy-start | bytes 3145732
  7.2 140.1 %reduce-scatter.5.cloned.1.call-start = ((), (), s32[]{:S(2)}) async-start(), calls=%async_computation.2 | async-start | bytes 2162688 | tf_op jit(solution)/shard_map/reduce_scatter | solution.py:37
  43.4 0.8 copy-start.1
  43.5 2650.1 %reduce-scatter.7.cloned.1.call-start = ((), (), s32[]{:S(2)}) async-start(), calls=%async_computation.3 | async-start | bytes 8404992
  44.3 10.9 collective-permute-start
  45.0 11.0 collective-permute-start.1
  153.1 0.8 copy-start.2
  153.1 2541.3 %copy-start.3 = (f32[4,32]{1,0:T(4,128)S(1)}, f32[4,32]{1,0:T(4,128)}, u32[]{:S(2)}) copy-start(f32[4,32]{1,0:T(4,128)} %param.7) | copy-start | bytes 1540
Sparse Core Ops, SparseCore 0:
  43.6 103.6 reduce-scatter.4
  153.3 2540.2 reduce-scatter.6

commit v2 on v0

v2 whole, which is shorter than its diff:
```python
import functools

import jax
import jax.numpy as jnp
from jax import lax
from jax.experimental import pallas as pl
from jax.experimental.pallas import tpu as pltpu
from jax.sharding import PartitionSpec as P

MESH = pl.DeviceIdType.MESH
F32 = jnp.float32
BF16 = jnp.bfloat16
STRIDE = 2


def kernel(
    inv, low, pat, col_out, upd_out,
    invs, lg, lown, rhs, pbuf, t1, d1, s1, c1, q1, t2, d2, s2, c2, cs, ubuf, urecv, wbuf, wrecv,
    inv_send, inv_recv, own_sem, ag_send, ag_recv, pt_send, pt_recv, low_send, low_recv,
    p1_send, p1_recv, p2_send, p2_recv, col_send, col_recv, col_local, u_send, u_recv, w_send, w_recv,
    row_sem, col_sem,
):
    p = lax.axis_index("prow")
    z = lax.axis_index("pcol")
    k = lax.rem(p, 2)
    q = lax.div(p, 2)
    x = lax.rem(q, 4)
    y = lax.div(q, 4)
    other = 1 - k

    def dev(yy, xx, kk, zz):
        return (lax.rem(yy + 8, 4) * 8 + lax.rem(xx + 8, 4) * 2 + kk, lax.rem(zz + 32, 16))

    def chip(qq, kk, zz):
        return (qq * 2 + kk, zz)

    partner = dev(y, x, other, z)

    def remote(src, dst, send, recv, to):
        return pltpu.make_async_remote_copy(
            src_ref=src, dst_ref=dst, send_sem=send, recv_sem=recv, device_id=to, device_id_type=MESH
        )

    def signal(sem, to):
        pl.semaphore_signal(sem, inc=1, device_id=to, device_id_type=MESH)

    barrier = pltpu.get_barrier_semaphore()
    near = [partner, dev(y, x + 1, k, z), dev(y, x - 1, k, z), dev(y + 1, x, k, z), dev(y - 1, x, k, z)]
    for hop in range(1, STRIDE + 1):
        near += [dev(y, x, k, z + hop), dev(y, x, k, z - hop)]
    for to in near:
        signal(barrier, to)
    pl.semaphore_wait(barrier, len(near))

    def rows(zz, first=0, count=4):
        return (pl.ds(4 * k + first, count), slice(None), pl.ds(pl.multiple_of(8 * zz, 8), 8), slice(None))

    sends = []

    def spread(src, piece, d, way, s):
        for hop in range(STRIDE, 0, -1):
            t = d + hop
            if t > 8:
                continue
            if STRIDE == 2 and d % 2 == 1:
                continue
            if t == 8:
                src_at, dst_at = src(2 * way, 2), piece(2 * way, 2)
            else:
                src_at, dst_at = src(0, 4), piece(0, 4)
            c = remote(src_at, dst_at, ag_send.at[way, t], ag_recv.at[way, t], dev(y, x, k, z + s * hop))
            c.start()
            sends.append(c)

    ways = ((0, 1), (1, -1))
    for way, s in ways:
        spread(lambda f, n: low.at[pl.ds(f, n)], lambda f, n: lg.at[rows(z, f, n)], 0, way, s)
    inv_out = remote(
        inv.at[pl.ds(4 * other, 4)], invs.at[:, pl.ds(4 * k, 4)], inv_send, inv_recv, partner
    )
    own_out = remote(low, lg.at[rows(z)], pt_send.at[0, 0], pt_recv.at[0, 0], partner)
    own_out.start()
    inv_out.start()
    own_in = pltpu.make_async_copy(low, lg.at[rows(z)], own_sem.at[0])
    own_in.start()
    inv_in = pltpu.make_async_copy(inv.at[pl.ds(4 * k, 4)], invs.at[:, pl.ds(4 * k, 4)], own_sem.at[1])
    inv_in.start()
    root = q == z

    @pl.when(root)
    def _():
        pltpu.make_async_copy(low, lown, low_recv).start()

    signal(row_sem, dev(y, x + 1, k, z))
    signal(row_sem, dev(y, x - 1, k, z))
    pl.semaphore_wait(row_sem, 2)
    for lap in range(2):
        signal(col_sem.at[lap], dev(y + 1, x, k, z))
        signal(col_sem.at[lap], dev(y - 1, x, k, z))
        pl.semaphore_wait(col_sem.at[lap], 2)

    forwards = [own_out]
    scatters = []

    def arrive(d):
        for way, s in ways:
            from_z = lax.rem(z - s * d + 32, 16)
            if d == 8:
                got = lg.at[rows(from_z, 2 * way, 2)]
            else:
                got = lg.at[rows(from_z)]
            remote(got, got, ag_send.at[way, d], ag_recv.at[way, d], partner).wait_recv()
            here = lambda f, n, fz=from_z: lg.at[rows(fz, f, n)]
            spread(here, here, d, way, s)
            c = remote(got, got, pt_send.at[way, d], pt_recv.at[way, d], partner)
            c.start()
            forwards.append(c)
            if d < 8 or way == 1:
                c = remote(
                    lg.at[rows(from_z)], lown, low_send.at[way, d], low_recv, chip(from_z, k, z)
                )
                scatters.append(c)
                pl.when(root)(c.start)

    order = (2, 1, 4, 3, 6, 5, 8, 7) if STRIDE == 2 else tuple(range(1, 9))
    for d in order:
        arrive(d)

    def rows_of(kk, zz, first, count):
        return (pl.ds(4 * kk + first, count), slice(None), pl.ds(pl.multiple_of(8 * zz, 8), 8), slice(None))

    got = lg.at[rows_of(other, z, 0, 4)]
    remote(got, got, pt_send.at[0, 0], pt_recv.at[0, 0], partner).wait_recv()
    for d in order:
        for way, s in ways:
            from_z = lax.rem(z - s * d + 32, 16)
            got = lg.at[rows_of(other, from_z, 2 * way, 2)] if d == 8 else lg.at[rows_of(other, from_z, 0, 4)]
            remote(got, got, pt_send.at[way, d], pt_recv.at[way, d], partner).wait_recv()
    own_in.wait()
    inv_in.wait()
    inv_out.wait_recv()

    def present(g):
        return jnp.sum((pat[...] == g).astype(F32), axis=1, keepdims=True)

    for j in range(8):
        keep = present(8 * q + j)
        for n in range(4):
            keep_n = jnp.broadcast_to(keep[n : n + 1, :], (128, 128)).astype(BF16)
            rhs[128 * j : 128 * (j + 1), 128 * n : 128 * (n + 1)] = lg[j, n] * keep_n

    def part(h, i, m):
        return pbuf.at[i, :, m] if h == 0 else pbuf.at[i, m]

    def mod4(v):
        return lax.rem(v + 8, 4)

    def ring(h, step):
        return (x if (h == 0) == (step == 1) else y)

    def ring_dev(h, step, by):
        return dev(y, x + by, k, z) if (h == 0) == (step == 1) else dev(y + by, x, k, z)

    reduces = []

    def begin(h, way, s, step, chunk, t, d, send, recv):
        n = ring(h, step)
        for what, src, dst, by in (
            (0, chunk(mod4(n + 2 * s)), t, s),
            (1, chunk(mod4(n - s)), d, -s),
        ):
            c = remote(src, dst.at[h, way], send.at[h, way, what], recv.at[h, way, what], ring_dev(h, step, by))
            c.start()
            reduces.append(c)

    def combine(h, way, s, step, chunk, t, sbuf, cbuf, send, recv):
        n = ring(h, step)
        ref = t.at[h, way]
        remote(ref, ref, send.at[h, way, 0], recv.at[h, way, 0], partner).wait_recv()
        sbuf[h, way] = t[h, way] + chunk(mod4(n + s))[...]
        c = remote(sbuf.at[h, way], cbuf.at[h, way], send.at[h, way, 2], recv.at[h, way, 2], ring_dev(h, step, s))
        c.start()
        reduces.append(c)

    def finish(h, way, step, chunk, d, cbuf, send, recv):
        n = ring(h, step)
        ref = d.at[h, way]
        remote(ref, ref, send.at[h, way, 1], recv.at[h, way, 1], partner).wait_recv()
        ref = cbuf.at[h, way]
        remote(ref, ref, send.at[h, way, 2], recv.at[h, way, 2], partner).wait_recv()
        return chunk(n)[...] + d[h, way] + cbuf[h, way]

    pairs = [(h, way, s) for way, s in ways for h in range(2)]
    for h, way, s in pairs:
        i = 2 * h + way
        lhs = jnp.concatenate([invs[i, j] for j in range(8)], axis=1)
        prod = jnp.dot(lhs, rhs[...], preferred_element_type=F32)
        pbuf[i] = prod.reshape(4, 4, 8, 512)
        begin(h, way, s, 1, functools.partial(part, h, i), t1, d1, p1_send, p1_recv)
    for h, way, s in pairs:
        combine(h, way, s, 1, functools.partial(part, h, 2 * h + way), t1, s1, c1, p1_send, p1_recv)
    for h, way, s in pairs:
        q1[h, way] = finish(h, way, 1, functools.partial(part, h, 2 * h + way), d1, c1, p1_send, p1_recv)
        begin(h, way, s, 2, lambda m, h=h, way=way: q1.at[h, way, m], t2, d2, p2_send, p2_recv)
    for h, way, s in pairs:
        combine(h, way, s, 2, lambda m, h=h, way=way: q1.at[h, way, m], t2, s2, c2, p2_send, p2_recv)
    columns = [None] * 4
    for h, way, s in pairs:
        i = 2 * h + way
        total = finish(h, way, 2, lambda m, h=h, way=way: q1.at[h, way, m], d2, c2, p2_send, p2_recv)
        keep = present(8 * z + 4 * k + i)
        keep_row = jnp.concatenate([jnp.broadcast_to(keep[n : n + 1, :], (8, 128)) for n in range(4)], axis=1)
        columns[i] = -keep_row * total

    remote(lown, lown, low_send.at[0, 0], low_recv, partner).wait_recv()
    for n in range(4):
        left = lown[:, n].astype(F32).reshape(32, 128)
        right = jnp.concatenate([columns[i][:, 128 * n : 128 * (n + 1)] for i in range(4)], axis=0)
        prod = lax.dot_general(
            left, right, (((0,), (0,)), ((), ())), precision=lax.Precision.HIGHEST, preferred_element_type=F32
        )
        ubuf[n] = prod.reshape(16, 8, 128)

    def u_copy(step):
        to = lax.rem(q + step, 16)
        return remote(ubuf.at[:, to], urecv.at[step], u_send.at[step], u_recv.at[step], chip(to, k, z))

    @pl.loop(1, 16)
    def _(step):
        u_copy(step).start()

    for half in range(2):
        for i in range(4):
            for n in range(4):
                cs[half, i, n] = columns[i][4 * half : 4 * half + 4, 128 * n : 128 * (n + 1)]
    col_move = pltpu.make_async_copy(cs.at[k], col_out.at[pl.ds(4 * k, 4)], col_local)
    col_move.start()
    col_pass = remote(cs.at[other], col_out.at[pl.ds(4 * k, 4)], col_send, col_recv, partner)
    col_pass.start()

    value = ubuf[:, q]
    for step in range(1, 16):
        u_copy(step).wait_recv()
        value = value + urecv[step]

    group = lax.broadcasted_iota(jnp.int32, (8, 128), 1) // 32
    for m in range(4):
        packed = jnp.zeros((8, 128), F32)
        for n in range(4):
            turned = value[n] if n == m else pltpu.roll(value[n], (32 * (n - m)) % 128, 1)
            packed = jnp.where(group == n, turned, packed)
        for r in range(8):
            wbuf[r // 4, 4 * (r % 4) + m] = packed[r : r + 1, :]

    def w_copy(flip, step):
        kk = k if flip == 0 else other
        zz = lax.rem(z + step, 16)
        return remote(
            wbuf.at[kk, zz], wrecv.at[flip, step], w_send.at[flip, step], w_recv.at[flip, step], chip(q, kk, zz)
        )

    w_copy(1, 0).start()

    @pl.loop(1, 16)
    def _(step):
        w_copy(0, step).start()
        w_copy(1, step).start()

    inv_out.wait_send()
    for c in sends + forwards + reduces:
        c.wait_send()
    for c in scatters:
        pl.when(root)(c.wait_send)

    @pl.loop(1, 16)
    def _(step):
        u_copy(step).wait_send()

    col_move.wait()
    col_pass.wait()

    total = wbuf[k, z]
    w_copy(1, 0).wait_recv()
    total = total + wrecv[1, 0]
    for step in range(1, 16):
        for flip in range(2):
            w_copy(flip, step).wait_recv()
            total = total + wrecv[flip, step]
    upd_out[...] = total
    w_copy(1, 0).wait_send()

    @pl.loop(1, 16)
    def _(step):
        w_copy(0, step).wait_send()
        w_copy(1, step).wait_send()


def per_device(inverse_blocks, lower_blocks, pattern, diag_inverse):
    any_spec = pl.BlockSpec(memory_space=pl.ANY)
    vmem_spec = pl.BlockSpec(memory_space=pltpu.VMEM)
    dma = pltpu.SemaphoreType.DMA
    column, update = pl.pallas_call(
        kernel,
        out_shape=(
            jax.ShapeDtypeStruct((8, 4, 4, 128), F32),
            jax.ShapeDtypeStruct((1, 128), F32),
        ),
        in_specs=[any_spec, any_spec, vmem_spec],
        out_specs=(any_spec, vmem_spec),
        scratch_shapes=[
            pltpu.VMEM((4, 8, 128, 128), BF16),
            pltpu.VMEM((8, 4, 128, 128), BF16),
            pltpu.VMEM((4, 4, 8, 128), BF16),
            pltpu.VMEM((1024, 512), BF16),
            pltpu.VMEM((4, 4, 4, 8, 512), F32),
            pltpu.VMEM((2, 2, 4, 8, 512), F32),
            pltpu.VMEM((2, 2, 4, 8, 512), F32),
            pltpu.VMEM((2, 2, 4, 8, 512), F32),
            pltpu.VMEM((2, 2, 4, 8, 512), F32),
            pltpu.VMEM((2, 2, 4, 8, 512), F32),
            pltpu.VMEM((2, 2, 8, 512), F32),
            pltpu.VMEM((2, 2, 8, 512), F32),
            pltpu.VMEM((2, 2, 8, 512), F32),
            pltpu.VMEM((2, 2, 8, 512), F32),
            pltpu.VMEM((2, 4, 4, 4, 128), F32),
            pltpu.VMEM((4, 16, 8, 128), F32),
            pltpu.VMEM((16, 4, 8, 128), F32),
            pltpu.VMEM((2, 16, 1, 128), F32),
            pltpu.VMEM((2, 16, 1, 128), F32),
            dma, dma, dma((2,)),
            dma((2, 9)), dma((2, 9)),
            dma((2, 9)), dma((2, 9)),
            dma((2, 9)), dma,
            dma((2, 2, 3)), dma((2, 2, 3)),
            dma((2, 2, 3)), dma((2, 2, 3)),
            dma, dma, dma,
            dma((16,)), dma((16,)),
            dma((2, 16)), dma((2, 16)),
            pltpu.SemaphoreType.REGULAR, pltpu.SemaphoreType.REGULAR((2,)),
        ],
        compiler_params=pltpu.CompilerParams(
            collective_id=0, has_side_effects=True, vmem_limit_bytes=32 * 1024 * 1024
        ),
    )(inverse_blocks, lower_blocks, pattern)
    return column, diag_inverse - update.reshape(4, 32)


def solution(mesh):
    placed = (
        P("pcol", "prow", None, None),
        P("prow", None, "pcol", None),
        P(),
        P(None, ("prow", "pcol")),
    )
    return jax.shard_map(
        per_device,
        mesh=mesh,
        in_specs=placed,
        out_specs=(P("pcol", None, "prow", None), P(None, ("prow", "pcol"))),
        check_vma=False,
    )
```

time: 767 us -> 69.4 us (0.09)
  waiting for transfers between devices: 707 us -> 0 us
  Pallas kernels: 0 us -> 63.3 us
  blocking collectives: 31.8 us -> 0 us
  between operations: 13.8 us -> 0.65 us
    psum x2 -> x0, waiting for transfers between devices: 603 us -> none  [the longest x1 467 us: per_device(): totals = lax.psum(partial_value, ('prow', 'pcol'))]
    reduce_scatter x1 -> x0, waiting for transfers between devices: 104 us -> none  [per_device(): lax.psum_scatter(jnp.einsum('ijrb,jkbe->rike', inverse_blocks, masked, pr...]
    pallas_call x0 -> x1, Pallas kernels: none -> 63.3 us  [per_device(): pl.pallas_call(kernel, out_shape=(jax.ShapeDtypeStruct((8, 4, 4, 128), F3...]
    all_gather x1 -> x0, blocking collectives: 31.8 us -> none  [per_device(): whole = lax.all_gather(lower_blocks, 'pcol', axis=2, tiled=True)]
  transfers between devices with their start and end apart: 3 -> 0, of which waited for: 3 -> 0; matrix products, arithmetic and copies ran while one was open for 1% -> 0% of each run, Pallas kernels for 0% -> 0%
where the time goes in v2:
time: 69.4 us; the launch traced here: 69.1 us
  Pallas kernels  63.3 us (91%)
  local copies, waits for them, and re-layouts  3.89 us (6%)
  other arithmetic  1.26 us (2%)
    pallas_call x1, Pallas kernels, per_device(): pl.pallas_call(kernel, out_shape=(jax.ShapeDtypeStruct((8, 4, 4, 128), F3...  63.3 us
    unnamed x9, local copies, waits for them, and re-layouts  3.29 us

profile of v2, /device:TPU:1, one launch (start us, length us, event | category | flops | bytes accessed | tf_op | source)
XLA Modules:
  0.0 69.1 jit_solution(8846648062078598599)
XLA Ops:
  0.6 0.0 copy-start
  0.6 1.2 %copy-done = bf16[8,4,128,128]{3,2,1,0:T(8,128)(2,1)S(1)} copy-done((bf16[8,4,128,128]{3,2,1,0:T(8,128)(2,1)S(1)}, bf16[8,4,128,128]{3,2,1,0:T(8,128)(2,1)}, u32[]{:S(2)}) %copy-start) | copy-done | bytes 1048600
  1.9 0.0 copy-start.1
  1.9 0.8 %copy-done.1 = bf16[4,4,8,128]{3,2,1,0:T(8,128)(2,1)S(1)} copy-done((bf16[4,4,8,128]{3,2,1,0:T(8,128)(2,1)S(1)}, bf16[4,4,8,128]{3,2,1,0:T(8,128)(2,1)}, u32[]{:S(2)}) %copy-start.1) | copy-done | bytes 32792
  2.6 0.0 copy-start.2
  2.6 0.7 copy-done.2
  3.3 63.3 %shard_map.59 = (f32[8,4,4,128]{3,2,1,0:T(4,128)S(1)}, f32[1,128]{1,0:T(1,128)S(1)}) custom-call(bf16[8,4,128,128]{3,2,1,0:T(8,128)(2,1)S(1)} %copy-done, bf16[4,4,8,128]{3,2,1,0:T(8,128)(2,1)S(1)} %copy-done.1, s32[4,64]{1,0:T(4,128)S(1)} %copy-done.2), custom_call_target="tpu_custom_call" | custom-call | tf_op jit(solution)/shard_map/pallas_call | solution.py:302
  66.6 0.5 broadcast.3
  67.1 0.0 copy-start.3
  67.1 0.7 reduce.3
  67.8 0.1 reshape.7
  67.9 0.0 copy-done.3
  67.9 0.6 sub.3
  68.5 0.6 copy.7
Async XLA Ops:
  0.6 1.2 %copy-start = (bf16[8,4,128,128]{3,2,1,0:T(8,128)(2,1)S(1)}, bf16[8,4,128,128]{3,2,1,0:T(8,128)(2,1)}, u32[]{:S(2)}) copy-start(bf16[8,4,128,128]{3,2,1,0:T(8,128)(2,1)} %inv.1) | copy-start | bytes 3145732
  1.9 0.8 %copy-start.1 = (bf16[4,4,8,128]{3,2,1,0:T(8,128)(2,1)S(1)}, bf16[4,4,8,128]{3,2,1,0:T(8,128)(2,1)}, u32[]{:S(2)}) copy-start(bf16[4,4,8,128]{3,2,1,0:T(8,128)(2,1)} %low.1) | copy-start | bytes 98308
  2.6 0.7 copy-start.2
  67.1 0.8 %copy-start.3 = (f32[4,32]{1,0:T(4,128)S(1)}, f32[4,32]{1,0:T(4,128)}, u32[]{:S(2)}) copy-start(f32[4,32]{1,0:T(4,128)} %param.7) | copy-start | bytes 1540

commit v3 on v2

--- a/solution.py
+++ b/solution.py
@@ -10,11 +10,12 @@
 MESH = pl.DeviceIdType.MESH
 F32 = jnp.float32
 BF16 = jnp.bfloat16
-STRIDE = 2
+TREE = {0: ((3, 3), (1, 1)), 3: ((6, 3), (4, 1), (2, -1)), 6: ((8, 2), (7, 1), (5, -1))}
 
 
 def kernel(
-    inv, low, pat, col_out, upd_out,
+    inv, low, pat_in, diag_in, col_out, upd_out,
+    pat, diag,
     invs, lg, lown, rhs, pbuf, t1, d1, s1, c1, q1, t2, d2, s2, c2, cs, ubuf, urecv, wbuf, wrecv,
     inv_send, inv_recv, own_sem, ag_send, ag_recv, pt_send, pt_recv, low_send, low_recv,
     p1_send, p1_recv, p2_send, p2_recv, col_send, col_recv, col_local, u_send, u_recv, w_send, w_recv,
@@ -46,24 +47,19 @@
 
     barrier = pltpu.get_barrier_semaphore()
     near = [partner, dev(y, x + 1, k, z), dev(y, x - 1, k, z), dev(y + 1, x, k, z), dev(y - 1, x, k, z)]
-    for hop in range(1, STRIDE + 1):
+    for hop in range(1, 4):
         near += [dev(y, x, k, z + hop), dev(y, x, k, z - hop)]
     for to in near:
         signal(barrier, to)
     pl.semaphore_wait(barrier, len(near))
 
     def rows(zz, first=0, count=4):
-        return (pl.ds(4 * k + first, count), slice(None), pl.ds(pl.multiple_of(8 * zz, 8), 8), slice(None))
+        return (k, zz, pl.ds(first, count))
 
     sends = []
 
     def spread(src, piece, d, way, s):
-        for hop in range(STRIDE, 0, -1):
-            t = d + hop
-            if t > 8:
-                continue
-            if STRIDE == 2 and d % 2 == 1:
-                continue
+        for t, hop in TREE.get(d, ()):
             if t == 8:
                 src_at, dst_at = src(2 * way, 2), piece(2 * way, 2)
             else:
@@ -85,6 +81,10 @@
     own_in.start()
     inv_in = pltpu.make_async_copy(inv.at[pl.ds(4 * k, 4)], invs.at[:, pl.ds(4 * k, 4)], own_sem.at[1])
     inv_in.start()
+    pat_move = pltpu.make_async_copy(pat_in, pat, own_sem.at[2])
+    pat_move.start()
+    diag_move = pltpu.make_async_copy(diag_in, diag, own_sem.at[3])
+    diag_move.start()
     root = q == z
 
     @pl.when(root)
@@ -122,12 +122,20 @@
                 scatters.append(c)
                 pl.when(root)(c.start)
 
-    order = (2, 1, 4, 3, 6, 5, 8, 7) if STRIDE == 2 else tuple(range(1, 9))
+    order = (3, 1, 6, 4, 2, 7, 5, 8)
     for d in order:
         arrive(d)
 
+
+    def drain_ag():
+        inv_out.wait_send()
+        for c in sends + forwards:
+            c.wait_send()
+        for c in scatters:
+            pl.when(root)(c.wait_send)
+
     def rows_of(kk, zz, first, count):
-        return (pl.ds(4 * kk + first, count), slice(None), pl.ds(pl.multiple_of(8 * zz, 8), 8), slice(None))
+        return (kk, zz, pl.ds(first, count))
 
     got = lg.at[rows_of(other, z, 0, 4)]
     remote(got, got, pt_send.at[0, 0], pt_recv.at[0, 0], partner).wait_recv()
@@ -138,6 +146,8 @@
             remote(got, got, pt_send.at[way, d], pt_recv.at[way, d], partner).wait_recv()
     own_in.wait()
     inv_in.wait()
+    pat_move.wait()
+    diag_move.wait()
     inv_out.wait_recv()
 
     def present(g):
@@ -146,8 +156,9 @@
     for j in range(8):
         keep = present(8 * q + j)
         for n in range(4):
-            keep_n = jnp.broadcast_to(keep[n : n + 1, :], (128, 128)).astype(BF16)
-            rhs[128 * j : 128 * (j + 1), 128 * n : 128 * (n + 1)] = lg[j, n] * keep_n
+            keep_n = jnp.broadcast_to(keep[n : n + 1, :], (128, 128))
+            block = lg[j // 4, :, j % 4, n].astype(F32).reshape(128, 128)
+            rhs[128 * j : 128 * (j + 1), 128 * n : 128 * (n + 1)] = (block * keep_n).astype(BF16)
 
     def part(h, i, m):
         return pbuf.at[i, :, m] if h == 0 else pbuf.at[i, m]
@@ -286,7 +297,8 @@
         for flip in range(2):
             w_copy(flip, step).wait_recv()
             total = total + wrecv[flip, step]
-    upd_out[...] = total
+    for n in range(4):
+        upd_out[n : n + 1, :] = diag[n : n + 1, :] - total[:, 32 * n : 32 * (n + 1)]
     w_copy(1, 0).wait_send()
 
     @pl.loop(1, 16)
@@ -296,20 +308,21 @@
 
 
 def per_device(inverse_blocks, lower_blocks, pattern, diag_inverse):
-    any_spec = pl.BlockSpec(memory_space=pl.ANY)
+    any_spec = pl.BlockSpec(memory_space=pltpu.HBM)
     vmem_spec = pl.BlockSpec(memory_space=pltpu.VMEM)
     dma = pltpu.SemaphoreType.DMA
     column, update = pl.pallas_call(
         kernel,
         out_shape=(
-            jax.ShapeDtypeStruct((8, 4, 4, 128), F32),
-            jax.ShapeDtypeStruct((1, 128), F32),
+            pltpu.VMEM((8, 4, 4, 128), F32),
+            pltpu.VMEM((4, 32), F32),
         ),
-        in_specs=[any_spec, any_spec, vmem_spec],
-        out_specs=(any_spec, vmem_spec),
+        in_specs=[any_spec] * 4,
+        out_specs=(vmem_spec, vmem_spec),
         scratch_shapes=[
+            pltpu.VMEM((4, 64), jnp.int32), pltpu.VMEM((4, 32), F32),
             pltpu.VMEM((4, 8, 128, 128), BF16),
-            pltpu.VMEM((8, 4, 128, 128), BF16),
+            pltpu.VMEM((2, 16, 4, 4, 8, 128), BF16),
             pltpu.VMEM((4, 4, 8, 128), BF16),
             pltpu.VMEM((1024, 512), BF16),
             pltpu.VMEM((4, 4, 4, 8, 512), F32),
@@ -327,7 +340,7 @@
             pltpu.VMEM((16, 4, 8, 128), F32),
             pltpu.VMEM((2, 16, 1, 128), F32),
             pltpu.VMEM((2, 16, 1, 128), F32),
-            dma, dma, dma((2,)),
+            dma, dma, dma((4,)),
             dma((2, 9)), dma((2, 9)),
             dma((2, 9)), dma((2, 9)),
             dma((2, 9)), dma,
@@ -339,10 +352,10 @@
             pltpu.SemaphoreType.REGULAR, pltpu.SemaphoreType.REGULAR((2,)),
         ],
         compiler_params=pltpu.CompilerParams(
-            collective_id=0, has_side_effects=True, vmem_limit_bytes=32 * 1024 * 1024
+            collective_id=0, has_side_effects=True
         ),
-    )(inverse_blocks, lower_blocks, pattern)
-    return column, diag_inverse - update.reshape(4, 32)
+    )(inverse_blocks, lower_blocks, pattern, diag_inverse)
+    return column, update
 
 
 def solution(mesh):

time: 69.4 us -> 62.8 us (0.905)
  local copies, waits for them, and re-layouts: 3.89 us -> 1.21 us
  Pallas kernels: 63.3 us -> 60.8 us
  other arithmetic: 1.26 us -> 0 us
    pallas_call x1, Pallas kernels: 63.3 us -> 60.8 us  [per_device(): pl.pallas_call(kernel, out_shape=(pltpu.VMEM((8, 4, 4, 128), F32), pltpu....]
    unnamed x9 -> x2, local copies, waits for them, and re-layouts: 3.29 us -> 1.21 us
where the time goes in v3:
time: 62.8 us; the launch traced here: 62.7 us
  Pallas kernels  60.8 us (97%)
  local copies, waits for them, and re-layouts  1.21 us (2%)
  between operations  0.64 us (1%)
    pallas_call x1, Pallas kernels, per_device(): pl.pallas_call(kernel, out_shape=(pltpu.VMEM((8, 4, 4, 128), F32), pltpu....  60.8 us

profile of v3, /device:TPU:1, one launch (start us, length us, event | category | flops | bytes accessed | tf_op | source)
XLA Modules:
  0.0 62.7 jit_solution(14679468331808523925)
XLA Ops:
  0.6 60.8 %shard_map.59 = (f32[8,4,4,128]{3,2,1,0:T(4,128)S(1)}, f32[4,32]{1,0:T(4,128)S(1)}) custom-call(bf16[8,4,128,128]{3,2,1,0:T(8,128)(2,1)} %inv.1, bf16[4,4,8,128]{3,2,1,0:T(8,128)(2,1)} %low.1, s32[4,64]{1,0:T(4,128)} %pat_in.1, f32[4,32]{1,0:T(4,128)} %diag_in.1), custom_call_target="tpu_custom_call" | custom-call | tf_op jit(solution)/shard_map/pallas_call | solution.py:314
  61.5 0.6 %copy.8 = f32[8,4,4,128]{3,2,1,0:T(4,128)} copy(f32[8,4,4,128]{3,2,1,0:T(4,128)S(1)} %get-tuple-element.2) | data formatting | bytes 131072
  62.1 0.6 copy.9

commit v4 on v3

--- a/solution.py
+++ b/solution.py
@@ -16,9 +16,9 @@
 def kernel(
     inv, low, pat_in, diag_in, col_out, upd_out,
     pat, diag,
-    invs, lg, lown, rhs, pbuf, t1, d1, s1, c1, q1, t2, d2, s2, c2, cs, ubuf, urecv, wbuf, wrecv,
+    invs, lg, lown, rhs, pbuf, t1, d1, s1, c1, q1, t2, d2, s2, c2, cs, lring, ubuf, urecv, wbuf, wrecv,
     inv_send, inv_recv, own_sem, ag_send, ag_recv, pt_send, pt_recv, low_send, low_recv,
-    p1_send, p1_recv, p2_send, p2_recv, col_send, col_recv, col_local, u_send, u_recv, w_send, w_recv,
+    p1_send, p1_recv, p2_send, p2_recv, col_send, col_recv, col_local, lr_send, lr_recv, u_send, u_recv, w_send, w_recv,
     row_sem, col_sem,
 ):
     p = lax.axis_index("prow")
@@ -210,35 +210,67 @@
         begin(h, way, s, 1, functools.partial(part, h, i), t1, d1, p1_send, p1_recv)
     for h, way, s in pairs:
         combine(h, way, s, 1, functools.partial(part, h, 2 * h + way), t1, s1, c1, p1_send, p1_recv)
+
+    remote(lown, lown, low_send.at[0, 0], low_recv, partner).wait_recv()
+    mine = (y, x)
+    shares = []
+    for h in range(2):
+        c = pltpu.make_async_copy(lown.at[pl.ds(2 * h, 2)], lring.at[h, :, mine[h]], lr_recv.at[h, 0])
+        c.start()
+        for by in (2, 1, 3):
+            to = dev(y + by, x, k, z) if h == 0 else dev(y, x + by, k, z)
+            c = remote(lown.at[pl.ds(2 * h, 2)], lring.at[h, :, mine[h]], lr_send.at[h, by], lr_recv.at[h, by], to)
+            c.start()
+            shares.append(c)
     for h, way, s in pairs:
         q1[h, way] = finish(h, way, 1, functools.partial(part, h, 2 * h + way), d1, c1, p1_send, p1_recv)
         begin(h, way, s, 2, lambda m, h=h, way=way: q1.at[h, way, m], t2, d2, p2_send, p2_recv)
+    for h in range(2):
+        for by in range(4):
+            ref = lring.at[h, :, mod4(mine[h] - by)]
+            if by == 0:
+                pltpu.make_async_copy(lown.at[pl.ds(2 * h, 2)], ref, lr_recv.at[h, 0]).wait()
+            else:
+                remote(ref, ref, lr_send.at[h, by], lr_recv.at[h, by], partner).wait_recv()
+    keeps = [present(8 * z + 4 * k + i) for i in range(4)]
+    for n in range(4):
+        left = lring[:, :, :, n].astype(F32).reshape(128, 128)
+        right = jnp.concatenate(
+            [
+                -jnp.broadcast_to(keeps[2 * h + way][n : n + 1, :], (32, 128))
+                * q1[h, way, :, :, 128 * n : 128 * (n + 1)].reshape(32, 128)
+                for h in range(2)
+                for way in range(2)
+            ],
+            axis=0,
+        )
+        prod = lax.dot_general(
+            left, right, (((0,), (0,)), ((), ())), precision=lax.Precision.HIGHEST, preferred_element_type=F32
+        )
+        ubuf[n] = prod.reshape(16, 8, 128)
+
+    def u_copy(dy, dx):
+        to_y, to_x = mod4(y + dy), mod4(x + dx)
+        slot = 4 * dy + dx
+        return remote(
+            ubuf.at[:, 4 * to_y + to_x], urecv.at[slot], u_send.at[slot], u_recv.at[slot], dev(to_y, to_x, k, z)
+        )
+
+    far = (0, 1, 2, 1)
+    u_order = sorted(((dy, dx) for dy in range(4) for dx in range(4) if dy + dx), key=lambda v: -far[v[0]] - far[v[1]])
+    u_sends = [u_copy(dy, dx) for dy, dx in u_order]
+    for c in u_sends:
+        c.start()
+
     for h, way, s in pairs:
         combine(h, way, s, 2, lambda m, h=h, way=way: q1.at[h, way, m], t2, s2, c2, p2_send, p2_recv)
     columns = [None] * 4
     for h, way, s in pairs:
         i = 2 * h + way
         total = finish(h, way, 2, lambda m, h=h, way=way: q1.at[h, way, m], d2, c2, p2_send, p2_recv)
-        keep = present(8 * z + 4 * k + i)
+        keep = keeps[i]
         keep_row = jnp.concatenate([jnp.broadcast_to(keep[n : n + 1, :], (8, 128)) for n in range(4)], axis=1)
         columns[i] = -keep_row * total
-
-    remote(lown, lown, low_send.at[0, 0], low_recv, partner).wait_recv()
-    for n in range(4):
-        left = lown[:, n].astype(F32).reshape(32, 128)
-        right = jnp.concatenate([columns[i][:, 128 * n : 128 * (n + 1)] for i in range(4)], axis=0)
-        prod = lax.dot_general(
-            left, right, (((0,), (0,)), ((), ())), precision=lax.Precision.HIGHEST, preferred_element_type=F32
-        )
-        ubuf[n] = prod.reshape(16, 8, 128)
-
-    def u_copy(step):
-        to = lax.rem(q + step, 16)
-        return remote(ubuf.at[:, to], urecv.at[step], u_send.at[step], u_recv.at[step], chip(to, k, z))
-
-    @pl.loop(1, 16)
-    def _(step):
-        u_copy(step).start()
 
     for half in range(2):
         for i in range(4):
@@ -250,9 +282,9 @@
     col_pass.start()
 
     value = ubuf[:, q]
-    for step in range(1, 16):
-        u_copy(step).wait_recv()
-        value = value + urecv[step]
+    for (dy, dx), c in zip(reversed(u_order), reversed(u_sends), strict=True):
+        c.wait_recv()
+        value = value + urecv[4 * dy + dx]
 
     group = lax.broadcasted_iota(jnp.int32, (8, 128), 1) // 32
     for m in range(4):
@@ -270,41 +302,28 @@
             wbuf.at[kk, zz], wrecv.at[flip, step], w_send.at[flip, step], w_recv.at[flip, step], chip(q, kk, zz)
         )
 
-    w_copy(1, 0).start()
-
-    @pl.loop(1, 16)
-    def _(step):
-        w_copy(0, step).start()
-        w_copy(1, step).start()
+    w_order = [(flip, step) for step in sorted(range(1, 16), key=lambda v: -min(v, 16 - v)) for flip in range(2)] + [(1, 0)]
+    w_sends = [w_copy(flip, step) for flip, step in w_order]
+    for c in w_sends:
+        c.start()
 
     inv_out.wait_send()
-    for c in sends + forwards + reduces:
+    for c in sends + forwards + reduces + shares + u_sends:
         c.wait_send()
     for c in scatters:
         pl.when(root)(c.wait_send)
 
-    @pl.loop(1, 16)
-    def _(step):
-        u_copy(step).wait_send()
-
     col_move.wait()
     col_pass.wait()
 
     total = wbuf[k, z]
-    w_copy(1, 0).wait_recv()
-    total = total + wrecv[1, 0]
-    for step in range(1, 16):
-        for flip in range(2):
-            w_copy(flip, step).wait_recv()
-            total = total + wrecv[flip, step]
+    for (flip, step), c in zip(reversed(w_order), reversed(w_sends), strict=True):
+        c.wait_recv()
+        total = total + wrecv[flip, step]
     for n in range(4):
         upd_out[n : n + 1, :] = diag[n : n + 1, :] - total[:, 32 * n : 32 * (n + 1)]
-    w_copy(1, 0).wait_send()
-
-    @pl.loop(1, 16)
-    def _(step):
-        w_copy(0, step).wait_send()
-        w_copy(1, step).wait_send()
+    for c in w_sends:
+        c.wait_send()
 
 
 def per_device(inverse_blocks, lower_blocks, pattern, diag_inverse):
@@ -336,6 +355,7 @@
             pltpu.VMEM((2, 2, 8, 512), F32),
             pltpu.VMEM((2, 2, 8, 512), F32),
             pltpu.VMEM((2, 4, 4, 4, 128), F32),
+            pltpu.VMEM((2, 2, 4, 4, 8, 128), BF16),
             pltpu.VMEM((4, 16, 8, 128), F32),
             pltpu.VMEM((16, 4, 8, 128), F32),
             pltpu.VMEM((2, 16, 1, 128), F32),
@@ -347,6 +367,7 @@
             dma((2, 2, 3)), dma((2, 2, 3)),
             dma((2, 2, 3)), dma((2, 2, 3)),
             dma, dma, dma,
+            dma((2, 4)), dma((2, 4)),
             dma((16,)), dma((16,)),
             dma((2, 16)), dma((2, 16)),
             pltpu.SemaphoreType.REGULAR, pltpu.SemaphoreType.REGULAR((2,)),

time: 62.8 us -> 58.3 us (0.928)
  Pallas kernels: 60.8 us -> 56.4 us
    pallas_call x1, Pallas kernels: 60.8 us -> 56.4 us  [per_device(): pl.pallas_call(kernel, out_shape=(pltpu.VMEM((8, 4, 4, 128), F32), pltpu....]
where the time goes in v4:
time: 58.3 us; the launch traced here: 58.2 us
  Pallas kernels  56.4 us (97%)
  local copies, waits for them, and re-layouts  1.21 us (2%)
  between operations  0.64 us (1%)
    pallas_call x1, Pallas kernels, per_device(): pl.pallas_call(kernel, out_shape=(pltpu.VMEM((8, 4, 4, 128), F32), pltpu....  56.4 us
    unnamed x2, local copies, waits for them, and re-layouts  1.21 us

profile of v4, /device:TPU:1, one launch (start us, length us, event | category | flops | bytes accessed | tf_op | source)
XLA Modules:
  0.0 58.2 jit_solution(8603631803442331694)
XLA Ops:
  0.6 56.4 %shard_map.59 = (f32[8,4,4,128]{3,2,1,0:T(4,128)S(1)}, f32[4,32]{1,0:T(4,128)S(1)}) custom-call(bf16[8,4,128,128]{3,2,1,0:T(8,128)(2,1)} %inv.1, bf16[4,4,8,128]{3,2,1,0:T(8,128)(2,1)} %low.1, s32[4,64]{1,0:T(4,128)} %pat_in.1, f32[4,32]{1,0:T(4,128)} %diag_in.1), custom_call_target="tpu_custom_call" | custom-call | tf_op jit(solution)/shard_map/pallas_call | solution.py:333
  57.0 0.6 %copy.8 = f32[8,4,4,128]{3,2,1,0:T(4,128)} copy(f32[8,4,4,128]{3,2,1,0:T(4,128)S(1)} %get-tuple-element.2) | data formatting | bytes 131072
  57.6 0.6 copy.9

commit v5 on v4

v5 whole, which is shorter than its diff:
```python
import functools

import jax
import jax.numpy as jnp
from jax import lax
from jax.experimental import pallas as pl
from jax.experimental.pallas import tpu as pltpu
from jax.sharding import PartitionSpec as P

MESH = pl.DeviceIdType.MESH
F32 = jnp.float32
BF16 = jnp.bfloat16
TREE = {0: ((3, 3), (1, 1)), 3: ((6, 3), (4, 1), (2, -1)), 6: ((8, 2), (7, 1), (5, -1))}

NW = 2
NN = 4 // NW
LANES = 512 // NW


def kernel(
    inv, low, pat_in, diag_in, col_out, upd_out,
    pat, diag,
    invs, lg, lown, rhs, masks, pbuf, t1, d1, s1, c1, q1, t2, d2, s2, c2, cs, lring, ubuf, urecv, wbuf, wrecv,
    sized, near_send, pass_send, sum_send, low_send, w_send,
    own_sem, pat_sem, ag_recv, pt_recv, low_recv, t1_recv, p1_recv, t2_recv, p2_recv, lr_recv, col_recv, u_recv, w_recv,
    row_sem, col_sem,
):
    p = lax.axis_index("prow")
    z = lax.axis_index("pcol")
    k = lax.rem(p, 2)
    q = lax.div(p, 2)
    x = lax.rem(q, 4)
    y = lax.div(q, 4)
    other = 1 - k

    def dev(yy, xx, kk, zz):
        return (lax.rem(yy + 8, 4) * 8 + lax.rem(xx + 8, 4) * 2 + kk, lax.rem(zz + 32, 16))

    def chip(qq, kk, zz):
        return (qq * 2 + kk, zz)

    partner = dev(y, x, other, z)

    def remote(src, dst, send, recv, to):
        return pltpu.make_async_remote_copy(
            src_ref=src, dst_ref=dst, send_sem=send, recv_sem=recv, device_id=to, device_id_type=MESH
        )

    def await_kib(sem, count):
        ref = sized.at[pl.ds(0, count)]
        pltpu.make_async_copy(ref, ref, sem).wait()

    def signal(sem, to):
        pl.semaphore_signal(sem, inc=1, device_id=to, device_id_type=MESH)

    barrier = pltpu.get_barrier_semaphore()
    near = [partner, dev(y, x + 1, k, z), dev(y, x - 1, k, z), dev(y + 1, x, k, z), dev(y - 1, x, k, z)]
    for hop in range(1, 4):
        near += [dev(y, x, k, z + hop), dev(y, x, k, z - hop)]
    for to in near:
        signal(barrier, to)
    pl.semaphore_wait(barrier, len(near))

    def rows(kk, zz, wave, first=0, count=4):
        return (
            pl.ds(4 * kk + first, count), pl.ds(NN * wave, NN), pl.ds(pl.multiple_of(8 * zz, 8), 8), slice(None)
        )

    def spread(zz, d, way, s, wave, held):
        for t, hop in TREE.get(d, ()):
            first, count = (2 * way, 2) if t == 8 else (0, 4)
            src = lg.at[rows(k, zz, wave, first, count)] if held else low.at[:, pl.ds(NN * wave, NN)]
            c = remote(
                src, lg.at[rows(k, zz, wave, first, count)],
                near_send, ag_recv.at[way, t - 1, wave], dev(y, x, k, z + s * hop),
            )
            yield c

    ways = ((0, 1), (1, -1))
    starts = [[list(spread(z, 0, way, s, wave, False)) for way, s in ways] for wave in range(NW)]
    for hop in range(2):
        for wave in range(NW):
            for way, _ in ways:
                starts[wave][way][hop].start()
    inv_out = remote(
        inv.at[pl.ds(4 * other, 4)], invs.at[:, pl.ds(4 * k, 4)], pass_send, pt_recv.at[0], partner
    )
    whole = (pl.ds(4 * k, 4), slice(None), pl.ds(pl.multiple_of(8 * z, 8), 8), slice(None))
    own_out = remote(low, lg.at[whole], pass_send, pt_recv.at[0], partner)
    own_out.start()
    inv_out.start()
    own_in = pltpu.make_async_copy(low, lg.at[whole], own_sem)
    own_in.start()
    inv_in = pltpu.make_async_copy(inv.at[pl.ds(4 * k, 4)], invs.at[:, pl.ds(4 * k, 4)], own_sem)
    inv_in.start()
    pat_move = pltpu.make_async_copy(pat_in, pat, pat_sem.at[0])
    pat_move.start()
    diag_move = pltpu.make_async_copy(diag_in, diag, pat_sem.at[1])
    diag_move.start()
    root = q == z

    @pl.when(root)
    def _():
        pltpu.make_async_copy(low, lown, low_recv).start()

    signal(row_sem, dev(y, x + 1, k, z))
    signal(row_sem, dev(y, x - 1, k, z))
    pl.semaphore_wait(row_sem, 2)
    for lap in range(2):
        signal(col_sem.at[lap], dev(y + 1, x, k, z))
        signal(col_sem.at[lap], dev(y - 1, x, k, z))
        pl.semaphore_wait(col_sem.at[lap], 2)

    def present(g):
        return jnp.broadcast_to(jnp.sum((pat[...] == g).astype(F32), axis=1, keepdims=True), (4, 128))

    pat_move.wait()
    for j in range(8):
        masks[j] = present(8 * q + j)
    for i in range(4):
        masks[8 + i] = present(8 * z + 4 * k + i)


    def arrive(d, wave):
        for way, s in ways:
            from_z = lax.rem(z - s * d + 32, 16)
            got = lg.at[rows(k, from_z, wave, 2 * way, 2)] if d == 8 else lg.at[rows(k, from_z, wave)]
            pltpu.make_async_copy(got, got, ag_recv.at[way, d - 1, wave]).wait()
            for c in spread(from_z, d, way, s, wave, True):
                c.start()
            c = remote(got, got, pass_send, pt_recv.at[wave], partner)
            c.start()
            if wave == NW - 1 and (d < 8 or way == 1):
                piece = (pl.ds(4 * k, 4), slice(None), pl.ds(pl.multiple_of(8 * from_z, 8), 8), slice(None))
                c = remote(lg.at[piece], lown, low_send, low_recv, chip(from_z, k, z))
                pl.when(root)(c.start)

    order = (3, 1, 6, 4, 2, 7, 5, 8)

    def part(h, i, wave, m):
        lanes = pl.ds(LANES * wave, LANES)
        return pbuf.at[i, :, m, :, lanes] if h == 0 else pbuf.at[i, m, :, :, lanes]

    def mod4(v):
        return lax.rem(v + 8, 4)

    def ring(h, step):
        return (x if (h == 0) == (step == 1) else y)

    def ring_dev(h, step, by):
        return dev(y, x + by, k, z) if (h == 0) == (step == 1) else dev(y + by, x, k, z)

    def begin(h, way, s, step, chunk, t, d, t_sem, sem):
        n = ring(h, step)
        remote(chunk(mod4(n + 2 * s)), t, sum_send, t_sem, ring_dev(h, step, s)).start()
        remote(chunk(mod4(n - s)), d, sum_send, sem, ring_dev(h, step, -s)).start()

    def combine(h, way, s, step, chunk, t, sbuf, cbuf, sem):
        n = ring(h, step)
        sbuf[...] = t[...] + chunk(mod4(n + s))[...]
        remote(sbuf, cbuf, sum_send, sem, ring_dev(h, step, s)).start()

    def finish(h, step, chunk, d, cbuf):
        return chunk(ring(h, step))[...] + d[...] + cbuf[...]

    pairs = [(h, way, s) for way, s in ways for h in range(2)]

    def product(wave):
        for j in range(8):
            for n in range(NN * wave, NN * wave + NN):
                keep = jnp.broadcast_to(masks[j, n : n + 1, :], (128, 128)).astype(BF16)
                rhs[wave, 128 * j : 128 * (j + 1), 128 * (n % NN) : 128 * (n % NN + 1)] = lg[j, n] * keep
        for way, s in ways:
            lhs = jnp.concatenate(
                [jnp.concatenate([invs[2 * h + way, j] for j in range(8)], axis=1) for h in range(2)], axis=0
            )
            prod = jnp.dot(lhs, rhs[wave], preferred_element_type=F32)
            for h in range(2):
                i = 2 * h + way
                pbuf[i, :, :, :, LANES * wave : LANES * (wave + 1)] = prod[128 * h : 128 * (h + 1)].reshape(4, 4, 8, LANES)
                begin(
                    h, way, s, 1, functools.partial(part, h, i, wave),
                    t1.at[wave, h, way], d1.at[wave, h, way], t1_recv.at[wave, h, way], p1_recv.at[wave],
                )

    for d in order[:5]:
        for wave in range(NW):
            arrive(d, wave)
    diag_move.wait()
    for wave in range(NW):
        for d in order[5:]:
            arrive(d, wave)
        if wave == 0:
            await_kib(own_sem, 32 + 512)
        await_kib(pt_recv.at[wave], 30 * 16 // NW + (32 + 512 if wave == 0 else 0))
        product(wave)
    for wave in range(NW):
        for h, way, s in pairs:
            await_kib(t1_recv.at[wave, h, way], 64 // NW)
            combine(
                h, way, s, 1, functools.partial(part, h, 2 * h + way, wave),
                t1.at[wave, h, way], s1.at[wave, h, way], c1.at[wave, h, way], p1_recv.at[wave],
            )

    pltpu.make_async_copy(lown, lown, low_recv).wait()
    mine = (y, x)
    for h in range(2):
        c = pltpu.make_async_copy(lown.at[pl.ds(2 * h, 2)], lring.at[h, :, mine[h]], lr_recv)
        c.start()
        for by in (2, 1, 3):
            to = dev(y + by, x, k, z) if h == 0 else dev(y, x + by, k, z)
            c = remote(lown.at[pl.ds(2 * h, 2)], lring.at[h, :, mine[h]], near_send, lr_recv, to)
            c.start()
    for wave in range(NW):
        await_kib(p1_recv.at[wave], 512 // NW)
    for h, way, s in pairs:
        for wave in range(NW):
            q1[h, way, :, :, LANES * wave : LANES * (wave + 1)] = finish(
                h, 1, functools.partial(part, h, 2 * h + way, wave), d1.at[wave, h, way], c1.at[wave, h, way]
            )
        begin(
            h, way, s, 2, lambda m, h=h, way=way: q1.at[h, way, m], t2.at[h, way], d2.at[h, way], t2_recv, p2_recv
        )
    await_kib(lr_recv, 128)
    for n in range(4):
        left = lring[:, :, :, n].astype(F32).reshape(128, 128)
        right = jnp.concatenate(
            [
                -jnp.broadcast_to(masks[8 + 2 * h + way, n : n + 1, :], (32, 128))
                * q1[h, way, :, :, 128 * n : 128 * (n + 1)].reshape(32, 128)
                for h in range(2)
                for way in range(2)
            ],
            axis=0,
        )
        prod = lax.dot_general(
            left, right, (((0,), (0,)), ((), ())), precision=lax.Precision.HIGHEST, preferred_element_type=F32
        )
        ubuf[n] = prod.reshape(16, 8, 128)

    def u_copy(dy, dx):
        to_y, to_x = mod4(y + dy), mod4(x + dx)
        slot = 4 * dy + dx - 1
        return remote(
            ubuf.at[:, 4 * to_y + to_x], urecv.at[slot], near_send, u_recv, dev(to_y, to_x, k, z)
        )

    far = (0, 1, 2, 1)
    u_order = sorted(((dy, dx) for dy in range(4) for dx in range(4) if dy + dx), key=lambda v: -far[v[0]] - far[v[1]])
    u_sends = [u_copy(dy, dx) for dy, dx in u_order]
    for c in u_sends:
        c.start()

    await_kib(t2_recv, 64)
    for h, way, s in pairs:
        combine(h, way, s, 2, lambda m, h=h, way=way: q1.at[h, way, m],
            t2.at[h, way], s2.at[h, way], c2.at[h, way], p2_recv)
    await_kib(p2_recv, 128)
    columns = [None] * 4
    for h, way, s in pairs:
        i = 2 * h + way
        total = finish(h, 2, lambda m, h=h, way=way: q1.at[h, way, m],
            d2.at[h, way], c2.at[h, way])
        keep_row = jnp.concatenate(
            [jnp.broadcast_to(masks[8 + i, n : n + 1, :], (8, 128)) for n in range(4)], axis=1
        )
        columns[i] = -keep_row * total

    for half in range(2):
        for i in range(4):
            for n in range(4):
                cs[half, i, n] = columns[i][4 * half : 4 * half + 4, 128 * n : 128 * (n + 1)]
    col_move = pltpu.make_async_copy(cs.at[k], col_out.at[pl.ds(4 * k, 4)], col_recv.at[0])
    col_move.start()
    col_pass = remote(cs.at[other], col_out.at[pl.ds(4 * k, 4)], near_send, col_recv.at[1], partner)
    col_pass.start()

    value = ubuf[:, q]
    await_kib(u_recv, 240)
    for slot in range(15):
        value = value + urecv[slot]

    group = lax.broadcasted_iota(jnp.int32, (8, 128), 1) // 32
    for m in range(4):
        packed = jnp.zeros((8, 128), F32)
        for n in range(4):
            turned = value[n] if n == m else pltpu.roll(value[n], (32 * (n - m)) % 128, 1)
            packed = jnp.where(group == n, turned, packed)
        for r in range(8):
            wbuf[r // 4, 4 * (r % 4) + m] = packed[r : r + 1, :]

    def w_copy(flip, step):
        kk = k if flip == 0 else other
        zz = lax.rem(z + step, 16)
        return remote(
            wbuf.at[kk, zz], wrecv.at[16 * flip + step - 1], w_send, w_recv, chip(q, kk, zz)
        )

    w_order = [(flip, step) for step in sorted(range(1, 16), key=lambda v: -min(v, 16 - v)) for flip in range(2)] + [(1, 0)]
    w_sends = [w_copy(flip, step) for flip, step in w_order]
    for c in w_sends:
        c.start()

    await_kib(near_send, 480 + 96 + 240 + 32)
    await_kib(pass_send, 512 + 512)
    await_kib(sum_send, 768 + 192)

    @pl.when(root)
    def _():
        await_kib(low_send, 480)

    col_move.wait()
    col_pass.wait_recv()

    pltpu.make_async_copy(wrecv, wrecv, w_recv).wait()
    total = wbuf[k, z]
    for slot in range(31):
        total = total + wrecv[slot]
    for n in range(4):
        upd_out[n : n + 1, :] = diag[n : n + 1, :] - total[:, 32 * n : 32 * (n + 1)]
    pltpu.make_async_copy(wrecv, wrecv, w_send).wait()


def per_device(inverse_blocks, lower_blocks, pattern, diag_inverse):
    any_spec = pl.BlockSpec(memory_space=pltpu.HBM)
    vmem_spec = pl.BlockSpec(memory_space=pltpu.VMEM)
    dma = pltpu.SemaphoreType.DMA
    column, update = pl.pallas_call(
        kernel,
        out_shape=(
            pltpu.VMEM((8, 4, 4, 128), F32),
            pltpu.VMEM((4, 32), F32),
        ),
        in_specs=[any_spec] * 4,
        out_specs=(vmem_spec, vmem_spec),
        scratch_shapes=[
            pltpu.VMEM((4, 64), jnp.int32), pltpu.VMEM((4, 32), F32),
            pltpu.VMEM((4, 8, 128, 128), BF16),
            pltpu.VMEM((8, 4, 128, 128), BF16),
            pltpu.VMEM((4, 4, 8, 128), BF16),
            pltpu.VMEM((NW, 1024, LANES), BF16),
            pltpu.VMEM((12, 4, 128), F32),
            pltpu.VMEM((4, 4, 4, 8, 512), F32),
            pltpu.VMEM((NW, 2, 2, 4, 8, LANES), F32),
            pltpu.VMEM((NW, 2, 2, 4, 8, LANES), F32),
            pltpu.VMEM((NW, 2, 2, 4, 8, LANES), F32),
            pltpu.VMEM((NW, 2, 2, 4, 8, LANES), F32),
            pltpu.VMEM((2, 2, 4, 8, 512), F32),
            pltpu.VMEM((2, 2, 8, 512), F32),
            pltpu.VMEM((2, 2, 8, 512), F32),
            pltpu.VMEM((2, 2, 8, 512), F32),
            pltpu.VMEM((2, 2, 8, 512), F32),
            pltpu.VMEM((2, 4, 4, 4, 128), F32),
            pltpu.VMEM((2, 2, 4, 4, 8, 128), BF16),
            pltpu.VMEM((4, 16, 8, 128), F32),
            pltpu.VMEM((15, 4, 8, 128), F32),
            pltpu.VMEM((2, 16, 1, 128), F32),
            pltpu.VMEM((31, 1, 128), F32),
            pltpu.VMEM((1024, 512), BF16),
            dma, dma, dma, dma, dma,
            dma, dma((2,)), dma((2, 8, NW)), dma((NW,)), dma,
            dma((NW, 2, 2)), dma((NW,)), dma, dma,
            dma, dma((2,)), dma, dma,
            pltpu.SemaphoreType.REGULAR, pltpu.SemaphoreType.REGULAR((2,)),
        ],
        compiler_params=pltpu.CompilerParams(
            collective_id=0, has_side_effects=True
        ),
    )(inverse_blocks, lower_blocks, pattern, diag_inverse)
    return column, update


def solution(mesh):
    placed = (
        P("pcol", "prow", None, None),
        P("prow", None, "pcol", None),
        P(),
        P(None, ("prow", "pcol")),
    )
    return jax.shard_map(
        per_device,
        mesh=mesh,
        in_specs=placed,
        out_specs=(P("pcol", None, "prow", None), P(None, ("prow", "pcol"))),
        check_vma=False,
    )
```

time: 58.3 us -> 55.7 us (0.955)
  Pallas kernels: 56.4 us -> 53.7 us
    pallas_call x1, Pallas kernels: 56.4 us -> 53.7 us  [per_device(): pl.pallas_call(kernel, out_shape=(pltpu.VMEM((8, 4, 4, 128), F32), pltpu....]
where the time goes in v5:
time: 55.7 us; the launch traced here: 55.5 us
  Pallas kernels  53.7 us (96%)
  local copies, waits for them, and re-layouts  1.21 us (2%)
  between operations  0.64 us (1%)
    pallas_call x1, Pallas kernels, per_device(): pl.pallas_call(kernel, out_shape=(pltpu.VMEM((8, 4, 4, 128), F32), pltpu....  53.7 us
    unnamed x2, local copies, waits for them, and re-layouts  1.21 us

profile of v5, /device:TPU:1, one launch (start us, length us, event | category | flops | bytes accessed | tf_op | source)
XLA Modules:
  0.0 55.5 jit_solution(11376130050343882486)
XLA Ops:
  0.6 53.7 %shard_map.59 = (f32[8,4,4,128]{3,2,1,0:T(4,128)S(1)}, f32[4,32]{1,0:T(4,128)S(1)}) custom-call(bf16[8,4,128,128]{3,2,1,0:T(8,128)(2,1)} %inv.1, bf16[4,4,8,128]{3,2,1,0:T(8,128)(2,1)} %low.1, s32[4,64]{1,0:T(4,128)} %pat_in.1, f32[4,32]{1,0:T(4,128)} %diag_in.1), custom_call_target="tpu_custom_call" | custom-call | tf_op jit(solution)/shard_map/pallas_call | solution.py:328
  54.3 0.6 %copy.8 = f32[8,4,4,128]{3,2,1,0:T(4,128)} copy(f32[8,4,4,128]{3,2,1,0:T(4,128)S(1)} %get-tuple-element.2) | data formatting | bytes 131072
  55.0 0.6 %copy.9 = f32[4,32]{1,0:T(4,128)} copy(f32[4,32]{1,0:T(4,128)S(1)} %get-tuple-element.3) | data formatting | bytes 1024

commit v6 on v5

--- a/solution.py
+++ b/solution.py
@@ -223,7 +223,7 @@
         )
     await_kib(lr_recv, 128)
     for n in range(4):
-        left = lring[:, :, :, n].astype(F32).reshape(128, 128)
+        left = lring[:, :, :, n].astype(F32).reshape(128, 128).astype(BF16)
         right = jnp.concatenate(
             [
                 -jnp.broadcast_to(masks[8 + 2 * h + way, n : n + 1, :], (32, 128))
@@ -233,9 +233,11 @@
             ],
             axis=0,
         )
-        prod = lax.dot_general(
-            left, right, (((0,), (0,)), ((), ())), precision=lax.Precision.HIGHEST, preferred_element_type=F32
-        )
+        prod = jnp.zeros((128, 128), F32)
+        for _ in range(3):
+            taken = right.astype(BF16)
+            prod = prod + lax.dot_general(left, taken, (((0,), (0,)), ((), ())), preferred_element_type=F32)
+            right = right - taken.astype(F32)
         ubuf[n] = prod.reshape(16, 8, 128)
 
     def u_copy(dy, dx):
@@ -255,6 +257,32 @@
     for h, way, s in pairs:
         combine(h, way, s, 2, lambda m, h=h, way=way: q1.at[h, way, m],
             t2.at[h, way], s2.at[h, way], c2.at[h, way], p2_recv)
+    value = ubuf[:, q]
+    await_kib(u_recv, 240)
+    for slot in range(15):
+        value = value + urecv[slot]
+
+    group = lax.broadcasted_iota(jnp.int32, (8, 128), 1) // 32
+    for m in range(4):
+        packed = jnp.zeros((8, 128), F32)
+        for n in range(4):
+            turned = value[n] if n == m else pltpu.roll(value[n], (32 * (n - m)) % 128, 1)
+            packed = jnp.where(group == n, turned, packed)
+        for r in range(8):
+            wbuf[r // 4, 4 * (r % 4) + m] = packed[r : r + 1, :]
+
+    def w_copy(flip, step):
+        kk = k if flip == 0 else other
+        zz = lax.rem(z + step, 16)
+        return remote(
+            wbuf.at[kk, zz], wrecv.at[16 * flip + step - 1], w_send, w_recv, chip(q, kk, zz)
+        )
+
+    w_order = [(flip, step) for step in sorted(range(1, 16), key=lambda v: -min(v, 16 - v)) for flip in range(2)] + [(1, 0)]
+    w_sends = [w_copy(flip, step) for flip, step in w_order]
+    for c in w_sends:
+        c.start()
+
     await_kib(p2_recv, 128)
     columns = [None] * 4
     for h, way, s in pairs:
@@ -274,32 +302,6 @@
     col_move.start()
     col_pass = remote(cs.at[other], col_out.at[pl.ds(4 * k, 4)], near_send, col_recv.at[1], partner)
     col_pass.start()
-
-    value = ubuf[:, q]
-    await_kib(u_recv, 240)
-    for slot in range(15):
-        value = value + urecv[slot]
-
-    group = lax.broadcasted_iota(jnp.int32, (8, 128), 1) // 32
-    for m in range(4):
-        packed = jnp.zeros((8, 128), F32)
-        for n in range(4):
-            turned = value[n] if n == m else pltpu.roll(value[n], (32 * (n - m)) % 128, 1)
-            packed = jnp.where(group == n, turned, packed)
-        for r in range(8):
-            wbuf[r // 4, 4 * (r % 4) + m] = packed[r : r + 1, :]
-
-    def w_copy(flip, step):
-        kk = k if flip == 0 else other
-        zz = lax.rem(z + step, 16)
-        return remote(
-            wbuf.at[kk, zz], wrecv.at[16 * flip + step - 1], w_send, w_recv, chip(q, kk, zz)
-        )
-
-    w_order = [(flip, step) for step in sorted(range(1, 16), key=lambda v: -min(v, 16 - v)) for flip in range(2)] + [(1, 0)]
-    w_sends = [w_copy(flip, step) for flip, step in w_order]
-    for c in w_sends:
-        c.start()
 
     await_kib(near_send, 480 + 96 + 240 + 32)
     await_kib(pass_send, 512 + 512)

time: 55.7 us -> 54.1 us (0.971)
  Pallas kernels: 53.7 us -> 52.1 us
    pallas_call x1, Pallas kernels: 53.7 us -> 52.1 us  [per_device(): pl.pallas_call(kernel, out_shape=(pltpu.VMEM((8, 4, 4, 128), F32), pltpu....]
where the time goes in v6:
time: 54.1 us; the launch traced here: 54 us
  Pallas kernels  52.1 us (96%)
  local copies, waits for them, and re-layouts  1.21 us (2%)
  between operations  0.64 us (1%)
    pallas_call x1, Pallas kernels, per_device(): pl.pallas_call(kernel, out_shape=(pltpu.VMEM((8, 4, 4, 128), F32), pltpu....  52.1 us
    unnamed x2, local copies, waits for them, and re-layouts  1.21 us

profile of v6, /device:TPU:1, one launch (start us, length us, event | category | flops | bytes accessed | tf_op | source)
XLA Modules:
  0.0 54.0 jit_solution(6255722925532182281)
XLA Ops:
  0.6 52.1 %shard_map.59 = (f32[8,4,4,128]{3,2,1,0:T(4,128)S(1)}, f32[4,32]{1,0:T(4,128)S(1)}) custom-call(bf16[8,4,128,128]{3,2,1,0:T(8,128)(2,1)} %inv.1, bf16[4,4,8,128]{3,2,1,0:T(8,128)(2,1)} %low.1, s32[4,64]{1,0:T(4,128)} %pat_in.1, f32[4,32]{1,0:T(4,128)} %diag_in.1), custom_call_target="tpu_custom_call" | custom-call | tf_op jit(solution)/shard_map/pallas_call | solution.py:330
  52.8 0.6 %copy.8 = f32[8,4,4,128]{3,2,1,0:T(4,128)} copy(f32[8,4,4,128]{3,2,1,0:T(4,128)S(1)} %get-tuple-element.2) | data formatting | bytes 131072
  53.4 0.6 %copy.9 = f32[4,32]{1,0:T(4,128)} copy(f32[4,32]{1,0:T(4,128)S(1)} %get-tuple-element.3) | data formatting | bytes 1024
